TPU v7x, 32 devices: a whole 2x2x4 slice. The times are simulated.
32 devices in a mesh: rep: 4 (over x, core), fsdp: 8 (over z, y).
Axes of the slice: x: 2, y: 2, z: 4, core: 2. Of those that a mesh axis runs over, the one named last changes fastest.
Arguments:
- tokens: bfloat16 [64, 512, 1024], P('rep', 'fsdp'), may hold values from -6 to 6
- cotangent: bfloat16 [64, 512, 1024], P('rep', 'fsdp'), may hold values from -6 to 6
- lengths: int32 [4, 16], P('rep'), may hold values from 1 to 512, as said below
- deal: int32 [4, 16], P('rep'), may hold values from 0 to 15, each once within a row
- norm_gain: bfloat16 [1024], P('fsdp'), may hold values from 0.099609375 to 1.8984375
- in_weight: bfloat16 [1024, 3072], P('fsdp'), may hold values from -0.1875 to 0.1875
- conv_weight: bfloat16 [1024, 3], P('fsdp'), may hold values from -3 to 3
- out_weight: bfloat16 [1024, 1024], P('fsdp'), may hold values from -0.1875 to 0.1875
- ffn_gain: bfloat16 [1024], P('fsdp'), may hold values from 0.099609375 to 1.8984375
- gate_weight: bfloat16 [1024, 4608], P('fsdp'), may hold values from -0.1875 to 0.1875
- up_weight: bfloat16 [1024, 4608], P('fsdp'), may hold values from -0.1875 to 0.1875
- down_weight: bfloat16 [4608, 1024], P('fsdp'), may hold values from -0.1875 to 0.1875
Outputs:
- block_out: bfloat16 [64, 512, 1024], P('rep', 'fsdp')
- block_grad: bfloat16 [64, 512, 1024], P('rep', 'fsdp')
- norm_gain_grad: float32 [1024], P('fsdp')
- in_grad: float32 [1024, 3072], P('fsdp')
- conv_grad: float32 [1024, 3], P('fsdp')
- out_grad: float32 [1024, 1024], P('fsdp')
- ffn_gain_grad: float32 [1024], P('fsdp')
- gate_grad: float32 [1024, 4608], P('fsdp')
- up_grad: float32 [1024, 4608], P('fsdp')
- down_grad: float32 [4608, 1024], P('fsdp')
Inputs may be any that keep to these rules, and one draw needn't show every extreme that they name: In each row, the 2 lengths of slots 2 i to 2 i + 1 sum to at most 768; in each row one such set sums to exactly 768 and holds a length of exactly 512. `deal`: each row is a permutation of the group's sequence numbers.
All inputs are finite; a program needn't handle non-finite values.
Results may differ from a plain program's by a relative error of at most 0.018.
Values may be sent and summed in bfloat16 or wider, within the bound.
A program may use at most 256 MiB of HBM per device.

v0:
```python
import jax
import jax.numpy as jnp
from jax import lax
from jax.sharding import PartitionSpec as P

EPS = 1e-05
F32 = jnp.float32
BF16 = jnp.bfloat16


def row_scale(values):
    return lax.rsqrt(jnp.mean(values * values, axis=-1, keepdims=True) + EPS)


def norm_back(grad_unit, unit_rows, scale_rows):
    return scale_rows * (
        grad_unit - unit_rows * jnp.mean(grad_unit * unit_rows, axis=-1, keepdims=True)
    )


def over_rows(left_side, right_side):
    return lax.dot_general(
        left_side, right_side, (((0,), (0,)), ((), ())), preferred_element_type=F32
    )


def over_cols(left_side, right_side):
    return lax.dot_general(
        left_side, right_side, (((1,), (1,)), ((), ())), preferred_element_type=F32
    )


def dot(left_side, right_side):
    return jnp.dot(left_side, right_side, preferred_element_type=F32)


def live_mask(lengths, deal, span):
    slots = jnp.arange(deal.shape[1], dtype=jnp.int32)
    picked = deal[0][:, None] == slots[None, :]
    source_len = jnp.sum(jnp.where(picked, lengths[0][:, None], 0), axis=0)
    position = lax.axis_index("fsdp") * span + jnp.arange(span, dtype=jnp.int32)
    return (position[None, :] < source_len[:, None]).astype(F32)[..., None]


def shift(values, amount):
    size = lax.axis_size("fsdp")
    pairs = [(i, i + amount) for i in range(size) if 0 <= i + amount < size]
    return lax.ppermute(values, "fsdp", pairs)


def body(
    tokens,
    cotangent,
    lengths,
    deal,
    norm_gain,
    in_weight,
    conv_weight,
    out_weight,
    ffn_gain,
    gate_weight,
    up_weight,
    down_weight,
):
    seqs, span, width = tokens.shape
    live = live_mask(lengths, deal, span)
    halo = shift(tokens[:, span - 2 :], 1)

    def gather(values):
        return lax.all_gather(values, "fsdp", axis=0, tiled=True)

    norm_gain, in_weight, conv_weight, out_weight = map(
        gather, (norm_gain, in_weight, conv_weight, out_weight)
    )
    ffn_gain, gate_weight, up_weight, down_weight = map(
        gather, (ffn_gain, gate_weight, up_weight, down_weight)
    )
    gain_one = norm_gain.astype(F32)
    gain_two = ffn_gain.astype(F32)
    taps = conv_weight.astype(F32)
    extended = jnp.concatenate([halo, tokens], axis=1).astype(F32)
    scale_ext = row_scale(extended)
    unit_ext = extended * scale_ext
    normed_ext = (unit_ext * gain_one).astype(BF16)
    projected = dot(normed_ext.reshape(-1, width), in_weight).reshape(seqs, span + 2, 3 * width)
    b_gate = projected[:, :, :width]
    c_gate = projected[:, 2:, width : 2 * width]
    x_value = projected[:, :, 2 * width :]
    product = b_gate * x_value
    lags = (product[:, :span], product[:, 1 : span + 1], product[:, 2:])
    convolved = taps[:, 0] * lags[0] + taps[:, 1] * lags[1] + taps[:, 2] * lags[2]
    gated = (c_gate * convolved).astype(BF16).reshape(-1, width)
    token_rows = tokens.astype(F32).reshape(-1, width)
    middle = token_rows + dot(gated, out_weight)
    scale_two = row_scale(middle)
    unit_two = middle * scale_two
    normed_two = (unit_two * gain_two).astype(BF16)
    grad_out = (cotangent.astype(F32) * live).reshape(-1, width)
    grad_ffn = grad_out.astype(BF16)
    gate_lin = dot(normed_two, gate_weight)
    up_lin = dot(normed_two, up_weight)
    sigma = jax.nn.sigmoid(gate_lin)
    hidden = (gate_lin * sigma * up_lin).astype(BF16)
    output = middle + dot(hidden, down_weight)
    down_grad = over_rows(hidden, grad_ffn)
    grad_hidden = over_cols(grad_ffn, down_weight)
    grad_gate = (grad_hidden * up_lin * sigma * (1.0 + gate_lin * (1.0 - sigma))).astype(BF16)
    grad_up = (grad_hidden * gate_lin * sigma).astype(BF16)
    gate_grad = over_rows(normed_two, grad_gate)
    up_grad = over_rows(normed_two, grad_up)
    grad_normed_two = over_cols(grad_gate, gate_weight) + over_cols(grad_up, up_weight)
    ffn_gain_grad = jnp.sum(grad_normed_two * unit_two, axis=0)
    grad_middle = grad_out + norm_back(grad_normed_two * gain_two, unit_two, scale_two)
    grad_mixed = grad_middle.astype(BF16)
    out_grad = over_rows(gated, grad_mixed)
    grad_gated = over_cols(grad_mixed, out_weight).reshape(seqs, span, width)
    grad_c = grad_gated * convolved
    grad_conv = grad_gated * c_gate
    conv_grad = jnp.stack([jnp.sum(grad_conv * lag, axis=(0, 1)) for lag in lags], axis=1)
    ahead = jnp.concatenate([grad_conv, shift(grad_conv[:, :2], -1)], axis=1)
    grad_product = (
        taps[:, 2] * ahead[:, :span]
        + taps[:, 1] * ahead[:, 1 : span + 1]
        + taps[:, 0] * ahead[:, 2:]
    )
    grad_projected = (
        jnp.concatenate(
            [grad_product * x_value[:, 2:], grad_c, grad_product * b_gate[:, 2:]], axis=2
        )
        .astype(BF16)
        .reshape(-1, 3 * width)
    )
    normed_one = normed_ext[:, 2:].reshape(-1, width)
    unit_one = unit_ext[:, 2:].reshape(-1, width)
    scale_one = scale_ext[:, 2:].reshape(-1, 1)
    in_grad = over_rows(normed_one, grad_projected)
    grad_normed_one = over_cols(grad_projected, in_weight)
    norm_gain_grad = jnp.sum(grad_normed_one * unit_one, axis=0)
    grad_tokens = grad_middle + norm_back(grad_normed_one * gain_one, unit_one, scale_one)

    def to_slots(rows):
        return (rows.reshape(seqs, span, width) * live).astype(BF16)

    def reduced(values):
        share = lax.psum_scatter(values.astype(BF16), "fsdp", scatter_dimension=0, tiled=True)
        return lax.psum(share, "rep").astype(F32)

    return (
        to_slots(output),
        to_slots(grad_tokens),
        *map(
            reduced,
            (
                norm_gain_grad,
                in_grad,
                conv_grad,
                out_grad,
                ffn_gain_grad,
                gate_grad,
                up_grad,
                down_grad,
            ),
        ),
    )


def solution(mesh):
    rows = P("rep", "fsdp", None)
    lists = P("rep", None)
    vector = P("fsdp")
    matrix = P("fsdp", None)
    return jax.shard_map(
        body,
        mesh=mesh,
        in_specs=(
            rows,
            rows,
            lists,
            lists,
            vector,
            matrix,
            matrix,
            matrix,
            vector,
            matrix,
            matrix,
            matrix,
        ),
        out_specs=(rows, rows, vector, matrix, matrix, matrix, vector, matrix, matrix, matrix),
        check_vma=False,
    )
```

profile of v0, /device:TPU:0, one launch (start us, length us, event | category | flops | bytes accessed | tf_op | source)
XLA Modules:
  0.0 1513.2 jit_solution(15626529436629893880)
XLA Ops:
  15.6 19.0 %all_gather.26 = bf16[1024,3]{0,1:T(4,128)(2,1)S(1)} all-gather(bf16[128,3]{0,1:T(4,128)(2,1)S(1)} %copy-done.37), channel_id=1, replica_groups=mesh['rep'=4,'fsdp'=8] {'fsdp'}, dimensions={0}, use_global_device_ids=true | all-gather | bytes 6912 | tf_op jit(solution)/shard_map/all_gather | solution.py:70
  39.3 16.4 %all-gather = bf16[8,1,128]{2,1,0:T(2,128)(2,1)S(1)} all-gather(bf16[1,1,128]{2,1,0:T(2,128)(2,1)S(1)} %bitcast.93), channel_id=1, replica_groups=mesh['rep'=4,'fsdp'=8] {'fsdp'}, dimensions={0}, use_global_device_ids=true | all-gather | bytes 2304 | tf_op jit(solution)/shard_map/all_gather | solution.py:70
  55.7 18.4 %all-gather.1 = bf16[8,1,128]{2,1,0:T(2,128)(2,1)S(1)} all-gather(bf16[1,1,128]{2,1,0:T(2,128)(2,1)S(1)} %bitcast.94), channel_id=1, replica_groups=mesh['rep'=4,'fsdp'=8] {'fsdp'}, dimensions={0}, use_global_device_ids=true | all-gather | bytes 2304 | tf_op jit(solution)/shard_map/all_gather | solution.py:70
  75.6 36.5 %all-gather.8.cloned.1.call-done = bf16[1024,3072]{1,0:T(8,128)(2,1)} async-done(((bf16[128,3072]{1,0:T(8,128)(2,1)}), bf16[1024,3072]{1,0:T(8,128)(2,1)}) %all-gather.8.cloned.1.call-update) | async-done | bytes 6291472 | tf_op jit(solution)/shard_map/all_gather | solution.py:70
  133.6 28.2 %all-gather.10.cloned.1.call-done = bf16[1024,1024]{1,0:T(8,128)(2,1)} async-done(((bf16[128,1024]{1,0:T(8,128)(2,1)}), bf16[1024,1024]{1,0:T(8,128)(2,1)}) %all-gather.10.cloned.1.call-update) | async-done | bytes 2097168 | tf_op jit(solution)/shard_map/all_gather | solution.py:70
  168.8 131.7 %all-gather.12.cloned.1.call-done = bf16[1024,4608]{1,0:T(8,128)(2,1)} async-done(((bf16[128,4608]{1,0:T(8,128)(2,1)}), bf16[1024,4608]{1,0:T(8,128)(2,1)}) %all-gather.12.cloned.1.call-update) | async-done | bytes 9437200 | tf_op jit(solution)/shard_map/all_gather | solution.py:70
  300.5 16.1 %fusion.35 = f32[1024,4608]{1,0:T(8,128)} fusion(bf16[1024,1024]{1,0:T(8,128)(2,1)S(1)} %multiply_convert_fusion.7, bf16[1024,4608]{1,0:T(8,128)(2,1)} %all-gather.12.cloned.1.call-done), kind=kOutput, calls=%fused_computation.84 | convolution fusion | flops 9663676416 | bytes 30408704 | tf_op jit(solution)/shard_map/dot_general | solution.py:34
  316.7 122.2 %all-gather.14.cloned.1.call-done = bf16[1024,4608]{1,0:T(8,128)(2,1)} async-done(((bf16[128,4608]{1,0:T(8,128)(2,1)}), bf16[1024,4608]{1,0:T(8,128)(2,1)}) %all-gather.14.cloned.1.call-update) | async-done | bytes 9437200 | tf_op jit(solution)/shard_map/all_gather | solution.py:70
  438.8 17.0 %fusion.36 = f32[1024,4608]{1,0:T(8,128)} fusion(bf16[1024,1024]{1,0:T(8,128)(2,1)} %copy-done.15, bf16[1024,4608]{1,0:T(8,128)(2,1)} %all-gather.14.cloned.1.call-done), kind=kOutput, calls=%fused_computation.85 | convolution fusion | flops 9663676416 | bytes 30408704 | tf_op jit(solution)/shard_map/dot_general | solution.py:34
  455.8 121.3 %all-gather.16.cloned.1.call-done = bf16[4608,1024]{1,0:T(8,128)(2,1)} async-done(((bf16[576,1024]{1,0:T(8,128)(2,1)}), bf16[4608,1024]{1,0:T(8,128)(2,1)}) %all-gather.16.cloned.1.call-update) | async-done | bytes 9437200 | tf_op jit(solution)/shard_map/all_gather | solution.py:70
  577.2 31.1 %multiply_convert_fusion = (bf16[1024,4608]{1,0:T(8,128)(2,1)}, bf16[1024,4608]{1,0:T(8,128)(2,1)}, bf16[1024,4608]{1,0:T(8,128)(2,1)}) fusion(f32[1024,4608]{1,0:T(8,128)} %fusion.35, f32[1024,4608]{1,0:T(8,128)} %fusion.36, bf16[1024,1024]{1,0:T(8,128)(2,1)S(1)} %copy-done.13, bf16[4608,1024]{1,0:T(8,128)(2,1)} %all-gather.16.cloned.1.call-done), kind=kOutput, calls=%fused_computation | convolution fusion | flops 9739173888 | bytes 77594624 | tf_op jit(solution)/shard_map/dot_general | solution.py:28
  608.2 16.1 %fusion.37 = f32[1024,1024]{1,0:T(8,128)} fusion(bf16[1024,4608]{1,0:T(8,128)(2,1)} %get-tuple-element.33, bf16[1024,4608]{1,0:T(8,128)(2,1)} %all-gather.12.cloned.1.call-done), kind=kOutput, calls=%fused_computation.86 | convolution fusion | flops 9663676416 | bytes 23068672 | tf_op jit(solution)/shard_map/dot_general | solution.py:28
  624.3 17.7 %multiply_reduce_fusion = (bf16[1024]{0:T(1024)(128)(2,1)}, f32[1024]{0:T(1024)S(1)}, f32[1024,1024]{1,0:T(8,128)S(1)}) fusion(f32[1024,1024]{1,0:T(8,128)S(1)} %copy-done.7, f32[1024]{0:T(1024)S(1)} %add_rsqrt_fusion.1, f32[1024]{0:T(1024)S(1)} %bitcast.85, f32[1024,1024]{1,0:T(8,128)} %fusion.37, bf16[1024,4608]{1,0:T(8,128)(2,1)} %get-tuple-element.32, ...), kind=kOutput, calls=%fused_computation.49 | convolution fusion | flops 9671014400 | bytes 31471616 | tf_op jit(solution)/shard_map/dot_general | solution.py:28
  689.1 16.4 %convolution_convert_fusion.1 = bf16[1024,4608]{1,0:T(8,128)(2,1)} fusion(bf16[1024,1024]{1,0:T(8,128)(2,1)} %copy-done.15, bf16[1024,4608]{1,0:T(8,128)(2,1)} %get-tuple-element.33), kind=kOutput, calls=%fused_computation.6 | convolution fusion | flops 9668395008 | bytes 20971520 | tf_op jit(solution)/shard_map/dot_general | solution.py:22
  705.6 16.6 %convolution_convert_fusion = bf16[1024,4608]{1,0:T(8,128)(2,1)} fusion(bf16[1024,1024]{1,0:T(8,128)(2,1)} %copy-done.15, bf16[1024,4608]{1,0:T(8,128)(2,1)} %get-tuple-element.32), kind=kOutput, calls=%fused_computation.5 | convolution fusion | flops 9668395008 | bytes 20971520 | tf_op jit(solution)/shard_map/dot_general | solution.py:22
  722.3 16.7 %convolution_convert_fusion.2 = bf16[4608,1024]{1,0:T(8,128)(2,1)} fusion(bf16[1024,4608]{1,0:T(8,128)(2,1)} %get-tuple-element.34, bf16[1024,1024]{1,0:T(8,128)(2,1)} %bitcast_convert_fusion.1), kind=kOutput, calls=%fused_computation.7 | convolution fusion | flops 9668395008 | bytes 20971520 | tf_op jit(solution)/shard_map/dot_general | solution.py:22
  746.4 17.6 %convolution_add_fusion.1 = f32[1024,1024]{1,0:T(8,128)} fusion(f32[1024,1024]{1,0:T(8,128)} %copy-done.6, bf16[1024,4608]{1,0:T(8,128)(2,1)} %get-tuple-element.34, bf16[4608,1024]{1,0:T(8,128)(2,1)} %all-gather.16.cloned.1.call-done), kind=kOutput, calls=%fused_computation.66 | convolution fusion | flops 9664724992 | bytes 27262976 | tf_op jit(solution)/shard_map/dot_general | solution.py:34
  764.8 19.7 %reduce-scatter.11.cloned.1.call-done = bf16[128,1024]{1,0:T(8,128)(2,1)} async-done(((bf16[1024,1024]{1,0:T(8,128)(2,1)}), bf16[128,1024]{1,0:T(8,128)(2,1)}) %reduce-scatter.11.cloned.1.call-update) | async-done | bytes 262160 | tf_op jit(solution)/shard_map/reduce_scatter | solution.py:145
  784.5 120.6 %reduce-scatter.9.cloned.1.call-done = bf16[128,3072]{1,0:T(8,128)(2,1)} async-done(((bf16[1024,3072]{1,0:T(8,128)(2,1)}), bf16[128,3072]{1,0:T(8,128)(2,1)}) %reduce-scatter.9.cloned.1.call-update) | async-done | bytes 786448 | tf_op jit(solution)/shard_map/reduce_scatter | solution.py:145
  905.1 166.1 %reduce-scatter.13.cloned.1.call-done = bf16[128,4608]{1,0:T(8,128)(2,1)} async-done(((bf16[1024,4608]{1,0:T(8,128)(2,1)}), bf16[128,4608]{1,0:T(8,128)(2,1)}) %reduce-scatter.13.cloned.1.call-update) | async-done | bytes 1179664 | tf_op jit(solution)/shard_map/reduce_scatter | solution.py:145
  1071.2 165.9 %reduce-scatter.15.cloned.1.call-done = bf16[128,4608]{1,0:T(8,128)(2,1)} async-done(((bf16[1024,4608]{1,0:T(8,128)(2,1)}), bf16[128,4608]{1,0:T(8,128)(2,1)}) %reduce-scatter.15.cloned.1.call-update) | async-done | bytes 1179664 | tf_op jit(solution)/shard_map/reduce_scatter | solution.py:145
  1237.0 166.0 %reduce-scatter.17.cloned.1.call-done = bf16[576,1024]{1,0:T(8,128)(2,1)} async-done(((bf16[4608,1024]{1,0:T(8,128)(2,1)}), bf16[576,1024]{1,0:T(8,128)(2,1)}) %reduce-scatter.17.cloned.1.call-update) | async-done | bytes 1179664 | tf_op jit(solution)/shard_map/reduce_scatter | solution.py:145
  1415.7 19.4 %all-reduce.2 = (bf16[1024]{0:T(1024)(128)(2,1)S(1)}, bf16[1024]{0:T(1024)(128)(2,1)S(1)}) all-reduce(bf16[1024]{0:T(1024)(128)(2,1)S(1)} %get-tuple-element.15, bf16[1024]{0:T(1024)(128)(2,1)S(1)} %copy-done.36), channel_id=2, replica_groups=mesh['rep'=4,'fsdp'=8] {'fsdp'}, use_global_device_ids=true, to_apply=%region_6.7.clone | all-reduce | flops 2048 | bytes 8192
  1452.1 45.5 %all-reduce.7.cloned.1.call-done = (bf16[128,3072]{1,0:T(8,128)(2,1)}, bf16[128,1024]{1,0:T(8,128)(2,1)}, bf16[128,4608]{1,0:T(8,128)(2,1)}, bf16[128,4608]{1,0:T(8,128)(2,1)}, bf16[576,1024]{1,0:T(8,128)(2,1)}) async-done(((bf16[128,3072]{1,0:T(8,128)(2,1)}, bf16[128,1024]{1,0:T(8,128)(2,1)}, bf16[128,4608]{1,0:T(8,128)(2,1)}, bf16[128,4608]{1,0:T(8,128)(2,1)}, bf16[576,1024]{1,0:T(8,128)(2,1)}), ...) | async-done | bytes 4587536 | tf_op jit(solution)/shard_map/psum | solution.py:146
  (174 shorter events, 135.4 us)
Async XLA Ops:
  7.2 27.5 %copy-start.42 = (s32[1,16]{1,0:T(1,128)S(1)}, s32[1,16]{1,0:T(1,128)}, u32[]{:S(2)}) copy-start(s32[1,16]{1,0:T(1,128)} %param.15) | copy-start | bytes 196
  7.2 104.9 %all-gather.8.cloned.1.call-start = ((), (), s32[]{:S(2)}) async-start(), calls=%async_computation.6 | async-start | bytes 7077888 | tf_op jit(solution)/shard_map/all_gather | solution.py:70
  8.0 153.8 %all-gather.10.cloned.1.call-start = ((), (), s32[]{:S(2)}) async-start(), calls=%async_computation.7 | async-start | bytes 2359296 | tf_op jit(solution)/shard_map/all_gather | solution.py:70
  8.7 291.8 %all-gather.12.cloned.1.call-start = ((), (), s32[]{:S(2)}) async-start(), calls=%async_computation.8 | async-start | bytes 10616832 | tf_op jit(solution)/shard_map/all_gather | solution.py:70
  9.4 429.4 %all-gather.14.cloned.1.call-start = ((), (), s32[]{:S(2)}) async-start(), calls=%async_computation.9 | async-start | bytes 10616832 | tf_op jit(solution)/shard_map/all_gather | solution.py:70
  10.0 567.1 %all-gather.16.cloned.1.call-start = ((), (), s32[]{:S(2)}) async-start(), calls=%async_computation.10 | async-start | bytes 10616832 | tf_op jit(solution)/shard_map/all_gather | solution.py:70
  10.6 753.3 %reduce-scatter.19.cloned.1.call-start = ((), (), s32[]{:S(2)}) async-start(), calls=%async_computation.16 | async-start | bytes 294912
  10.7 63.3 %collective-permute-start = (bf16[16,2,1024]{2,1,0:T(2,128)(2,1)S(1)}, bf16[16,2,1024]{2,1,0:T(2,128)(2,1)S(1)}, u32[]{:S(2)}, u32[]{:S(2)}) collective-permute-start(bf16[16,2,1024]{2,1,0:T(2,128)(2,1)S(1)} %slice.59), channel_id=1, source_target_pairs={{0,1},{1,2},{2,3},{3,4},{4,5},{5,6},{6,7},{8,9},{9,10},{10,11},{11... | collective-permute-start | bytes 196616 | tf_op jit(solution)/shard_map/ppermute | solution.py:48
  37.4 37.7 %copy-start.2 = (f32[16,64,1024]{2,1,0:T(8,128)}, f32[16,64,1024]{2,1,0:T(8,128)S(1)}, u32[]{:S(2)}) copy-start(f32[16,64,1024]{2,1,0:T(8,128)S(1)} %convert_multiply_fusion.2) | copy-start | bytes 12582916
  39.2 85.9 %copy-start.27 = (f32[1024,1]{0,1:T(1,128)}, f32[1024,1]{0,1:T(1,128)S(1)}, u32[]{:S(2)}) copy-start(f32[1024,1]{0,1:T(1,128)S(1)} %get-tuple-element.42) | copy-start | bytes 12292
  39.3 85.9 %copy-start.29 = (f32[1024,1]{0,1:T(1,128)}, f32[1024,1]{0,1:T(1,128)S(1)}, u32[]{:S(2)}) copy-start(f32[1024,1]{0,1:T(1,128)S(1)} %get-tuple-element.43) | copy-start | bytes 12292
  39.3 85.9 %copy-start.31 = (f32[1024,1]{0,1:T(1,128)}, f32[1024,1]{0,1:T(1,128)S(1)}, u32[]{:S(2)}) copy-start(f32[1024,1]{0,1:T(1,128)S(1)} %get-tuple-element.44) | copy-start | bytes 12292
  55.7 67.8 %copy-start.25 = (f32[8,1,128]{2,1,0:T(1,128)}, f32[8,1,128]{2,1,0:T(1,128)S(1)}, u32[]{:S(2)}) copy-start(f32[8,1,128]{2,1,0:T(1,128)S(1)} %convert_element_type.136) | copy-start | bytes 12292
  74.1 49.5 %copy-start.20 = (bf16[16,2,1024]{2,1,0:T(2,128)(2,1)}, bf16[16,2,1024]{2,1,0:T(2,128)(2,1)S(1)}, u32[]{:S(2)}) copy-start(bf16[16,2,1024]{2,1,0:T(2,128)(2,1)S(1)} %collective-permute-done) | copy-start | bytes 196612
  75.6 47.9 %copy-start.33 = (f32[16,66]{1,0:T(8,128)}, f32[16,66]{1,0:T(8,128)S(1)}, u32[]{:S(2)}) copy-start(f32[16,66]{1,0:T(8,128)S(1)} %get-tuple-element.41) | copy-start | bytes 12676
  168.8 131.7 %copy-start.15 = (bf16[1024,1024]{1,0:T(8,128)(2,1)}, bf16[1024,1024]{1,0:T(8,128)(2,1)S(1)}, u32[]{:S(2)}) copy-start(bf16[1024,1024]{1,0:T(8,128)(2,1)S(1)} %multiply_convert_fusion.7) | copy-start | bytes 6291460
  316.7 260.5 %copy-start.13 = (bf16[1024,1024]{1,0:T(8,128)(2,1)S(1)}, bf16[1024,1024]{1,0:T(8,128)(2,1)}, u32[]{:S(2)}) copy-start(bf16[1024,1024]{1,0:T(8,128)(2,1)} %bitcast_convert_fusion.1) | copy-start | bytes 6291460
  654.8 129.7 %reduce-scatter.11.cloned.1.call-start = ((), (), s32[]{:S(2)}) async-start(), calls=%async_computation.12 | async-start | bytes 2359296 | tf_op jit(solution)/shard_map/reduce_scatter | solution.py:145
  661.6 243.5 %reduce-scatter.9.cloned.1.call-start = ((), (), s32[]{:S(2)}) async-start(), calls=%async_computation.11 | async-start | bytes 7077888 | tf_op jit(solution)/shard_map/reduce_scatter | solution.py:145
  662.8 7.1 collective-permute-start.1
  689.1 382.1 %reduce-scatter.13.cloned.1.call-start = ((), (), s32[]{:S(2)}) async-start(), calls=%async_computation.13 | async-start | bytes 10616832 | tf_op jit(solution)/shard_map/reduce_scatter | solution.py:145
  705.6 531.4 %reduce-scatter.15.cloned.1.call-start = ((), (), s32[]{:S(2)}) async-start(), calls=%async_computation.14 | async-start | bytes 10616832 | tf_op jit(solution)/shard_map/reduce_scatter | solution.py:145
  722.3 680.8 %reduce-scatter.17.cloned.1.call-start = ((), (), s32[]{:S(2)}) async-start(), calls=%async_computation.15 | async-start | bytes 10616832 | tf_op jit(solution)/shard_map/reduce_scatter | solution.py:145
  739.1 758.4 %all-reduce.7.cloned.1.call-start = ((), (), s32[]{:S(2)}) async-start(), calls=%async_computation.17 | async-start | bytes 9175040 | tf_op jit(solution)/shard_map/psum | solution.py:146
  (36 other events, 245.6 us)
Sparse Core Ops, SparseCore 0:
  10.2 101.8 all-gather.7
  114.2 47.4 all-gather.9
  163.9 136.5 all-gather.11
  302.6 136.2 all-gather.13
  440.9 136.2 all-gather.15
  654.9 59.4 reduce-scatter.18
  717.9 66.6 reduce-scatter.10
  788.1 116.9 reduce-scatter.8
  908.7 162.4 reduce-scatter.12
  1074.6 162.3 reduce-scatter.14
  1240.6 162.3 reduce-scatter.16
  1405.6 91.8 all-reduce.6
where the time goes:
time: 1520 us; the launch traced here: 1510 us
  waiting for transfers between devices  1130 us (74%)
  matrix products  212 us (14%)
  blocking collectives  79.7 us (5%)
  other arithmetic  49.1 us (3%)
  local copies, waits for them, and re-layouts  20.6 us (1%)
  between operations  15.7 us (1%)
    reduce_scatter x5, waiting for transfers between devices, reduced(): lax.psum_scatter(values.astype(BF16), 'fsdp', scatter_dimension=0, tiled=...  638 us
    all_gather x5, waiting for transfers between devices, gather(): return lax.all_gather(values, 'fsdp', axis=0, tiled=True)  440 us
    dot_general x5, matrix products, over_cols(): lax.dot_general(left_side, right_side, (((1,), (1,)), ((), ())), preferre...  79.8 us
    dot_general x5, matrix products, dot(): return jnp.dot(left_side, right_side, preferred_element_type=F32)  66.7 us
    dot_general x5, matrix products, over_rows(): lax.dot_general(left_side, right_side, (((0,), (0,)), ((), ())), preferre...  65.9 us
    all_gather x3, blocking collectives, gather(): return lax.all_gather(values, 'fsdp', axis=0, tiled=True)  53.8 us
    psum x1, waiting for transfers between devices, reduced(): return lax.psum(share, 'rep').astype(F32)  45.5 us
  transfers between devices with their start and end apart: 14, of which 12 were waited for; matrix products, arithmetic and copies ran while one was open for 12% of the time, Pallas kernels for 0%

commit v1 on v0

--- a/solution.py
+++ b/solution.py
@@ -2,10 +2,16 @@
 import jax.numpy as jnp
 from jax import lax
 from jax.sharding import PartitionSpec as P
+from jax.lax import all_gather
 
 EPS = 1e-05
 F32 = jnp.float32
 BF16 = jnp.bfloat16
+
+
+def compute_the_limits(buf, along_axis):
+    oldest = jnp.sum(all_gather(buf, along_axis), 0)
+    return oldest
 
 
 def row_scale(values):
@@ -143,7 +149,7 @@
 
     def reduced(values):
         share = lax.psum_scatter(values.astype(BF16), "fsdp", scatter_dimension=0, tiled=True)
-        return lax.psum(share, "rep").astype(F32)
+        return compute_the_limits(share, "rep").astype(F32)
 
     return (
         to_slots(output),

time: 1520 us -> 1580 us (1.039)
  waiting for transfers between devices: 1130 us -> 1170 us
    all_gather x0 -> x5, waiting for transfers between devices: none -> 89.1 us  [compute_the_limits(): oldest = jnp.sum(all_gather(buf, along_axis), 0)]
    reduce_scatter x5, waiting for transfers between devices: 638 us -> 592 us  [reduced(): lax.psum_scatter(values.astype(BF16), 'fsdp', scatter_dimension=0, tiled=...]
    psum x1 -> x0, waiting for transfers between devices: 45.5 us -> none  [reduced(): return lax.psum(share, 'rep').astype(F32)]
    unnamed x13 -> x17, waiting for transfers between devices: 3.23 us -> 43.9 us
  transfers between devices with their start and end apart: 14 -> 18, of which waited for: 12 -> 14; matrix products, arithmetic and copies ran while one was open for 12% -> 13% of each run, Pallas kernels for 0% -> 0%
where the time goes in v1:
time: 1580 us
  waiting for transfers between devices  1170 us (74%)
  matrix products  215 us (14%)
  blocking collectives  88.5 us (6%)
  other arithmetic  64.4 us (4%)
  local copies, waits for them, and re-layouts  19.3 us (1%)
    reduce_scatter x5, waiting for transfers between devices, reduced(): lax.psum_scatter(values.astype(BF16), 'fsdp', scatter_dimension=0, tiled=...  592 us
    all_gather x5, waiting for transfers between devices, gather(): return lax.all_gather(values, 'fsdp', axis=0, tiled=True)  440 us
    all_gather x5, waiting for transfers between devices, compute_the_limits(): oldest = jnp.sum(all_gather(buf, along_axis), 0)  89.1 us
    dot_general x5, matrix products, over_cols(): lax.dot_general(left_side, right_side, (((1,), (1,)), ((), ())), preferre...  84.8 us
    dot_general x5, matrix products, dot(): return jnp.dot(left_side, right_side, preferred_element_type=F32)  66.5 us
    dot_general x5, matrix products, over_rows(): lax.dot_general(left_side, right_side, (((0,), (0,)), ((), ())), preferre...  63.4 us
    all_gather x3, blocking collectives, gather(): return lax.all_gather(values, 'fsdp', axis=0, tiled=True)  53.7 us
    unnamed x17, waiting for transfers between devices  43.9 us
  transfers between devices with their start and end apart: 18, of which 14 were waited for; matrix products, arithmetic and copies ran while one was open for 13% of the time, Pallas kernels for 0%

profile of v1, /device:TPU:0, one launch (start us, length us, event | category | flops | bytes accessed | tf_op | source)
XLA Modules:
  0.0 1575.2 jit_solution(3971152655006084069)
XLA Ops:
  15.6 19.0 %all_gather.74 = bf16[1024,3]{0,1:T(4,128)(2,1)S(1)} all-gather(bf16[128,3]{0,1:T(4,128)(2,1)S(1)} %copy-done.32), channel_id=1, replica_groups=mesh['rep'=4,'fsdp'=8] {'fsdp'}, dimensions={0}, use_global_device_ids=true | all-gather | bytes 6912 | tf_op jit(solution)/shard_map/all_gather | solution.py:76
  39.3 16.4 %all-gather.8 = bf16[8,1,128]{2,1,0:T(2,128)(2,1)S(1)} all-gather(bf16[1,1,128]{2,1,0:T(2,128)(2,1)S(1)} %bitcast.109), channel_id=1, replica_groups=mesh['rep'=4,'fsdp'=8] {'fsdp'}, dimensions={0}, use_global_device_ids=true | all-gather | bytes 2304 | tf_op jit(solution)/shard_map/all_gather | solution.py:76
  55.6 18.4 %all-gather.9 = bf16[8,1,128]{2,1,0:T(2,128)(2,1)S(1)} all-gather(bf16[1,1,128]{2,1,0:T(2,128)(2,1)S(1)} %bitcast.110), channel_id=1, replica_groups=mesh['rep'=4,'fsdp'=8] {'fsdp'}, dimensions={0}, use_global_device_ids=true | all-gather | bytes 2304 | tf_op jit(solution)/shard_map/all_gather | solution.py:76
  75.6 36.5 %all-gather.23.cloned.1.call-done = bf16[1024,3072]{1,0:T(8,128)(2,1)} async-done(((bf16[128,3072]{1,0:T(8,128)(2,1)}), bf16[1024,3072]{1,0:T(8,128)(2,1)}) %all-gather.23.cloned.1.call-update) | async-done | bytes 6291472 | tf_op jit(solution)/shard_map/all_gather | solution.py:76
  133.5 28.2 %all-gather.25.cloned.1.call-done = bf16[1024,1024]{1,0:T(8,128)(2,1)} async-done(((bf16[128,1024]{1,0:T(8,128)(2,1)}), bf16[1024,1024]{1,0:T(8,128)(2,1)}) %all-gather.25.cloned.1.call-update) | async-done | bytes 2097168 | tf_op jit(solution)/shard_map/all_gather | solution.py:76
  168.8 131.7 %all-gather.27.cloned.1.call-done = bf16[1024,4608]{1,0:T(8,128)(2,1)} async-done(((bf16[128,4608]{1,0:T(8,128)(2,1)}), bf16[1024,4608]{1,0:T(8,128)(2,1)}) %all-gather.27.cloned.1.call-update) | async-done | bytes 9437200 | tf_op jit(solution)/shard_map/all_gather | solution.py:76
  316.6 122.2 %all-gather.29.cloned.1.call-done = bf16[1024,4608]{1,0:T(8,128)(2,1)} async-done(((bf16[128,4608]{1,0:T(8,128)(2,1)}), bf16[1024,4608]{1,0:T(8,128)(2,1)}) %all-gather.29.cloned.1.call-update) | async-done | bytes 9437200 | tf_op jit(solution)/shard_map/all_gather | solution.py:76
  438.8 16.9 %fusion.36 = f32[1024,4608]{1,0:T(8,128)} fusion(bf16[1024,1024]{1,0:T(8,128)(2,1)} %copy-done.14, bf16[1024,4608]{1,0:T(8,128)(2,1)} %all-gather.29.cloned.1.call-done), kind=kOutput, calls=%fused_computation.87 | convolution fusion | flops 9663676416 | bytes 30408704 | tf_op jit(solution)/shard_map/dot_general | solution.py:40
  455.8 121.4 %all-gather.31.cloned.1.call-done = bf16[4608,1024]{1,0:T(8,128)(2,1)} async-done(((bf16[576,1024]{1,0:T(8,128)(2,1)}), bf16[4608,1024]{1,0:T(8,128)(2,1)}) %all-gather.31.cloned.1.call-update) | async-done | bytes 9437200 | tf_op jit(solution)/shard_map/all_gather | solution.py:76
  577.2 30.9 %multiply_convert_fusion = (bf16[1024,4608]{1,0:T(8,128)(2,1)}, bf16[1024,4608]{1,0:T(8,128)(2,1)}, bf16[1024,4608]{1,0:T(8,128)(2,1)}) fusion(f32[1024,4608]{1,0:T(8,128)} %fusion.35, f32[1024,4608]{1,0:T(8,128)} %fusion.36, bf16[1024,1024]{1,0:T(8,128)(2,1)S(1)} %copy-done.12, bf16[4608,1024]{1,0:T(8,128)(2,1)} %all-gather.31.cloned.1.call-done), kind=kOutput, calls=%fused_computation | convolution fusion | flops 9739173888 | bytes 77594624 | tf_op jit(solution)/shard_map/dot_general | solution.py:34
  624.1 17.7 %multiply_reduce_fusion = (bf16[1024]{0:T(1024)(128)(2,1)}, f32[1024]{0:T(1024)S(1)}, f32[1024,1024]{1,0:T(8,128)S(1)}) fusion(f32[1024,1024]{1,0:T(8,128)S(1)} %copy-done.6, f32[1024]{0:T(1024)S(1)} %add_rsqrt_fusion.1, f32[1024]{0:T(1024)S(1)} %bitcast.101, f32[1024,1024]{1,0:T(8,128)} %fusion.37, bf16[1024,4608]{1,0:T(8,128)(2,1)} %get-tuple-element.24, ...), kind=kOutput, calls=%fused_computation.49 | convolution fusion | flops 9671014400 | bytes 31471616 | tf_op jit(solution)/shard_map/dot_general | solution.py:34
  689.9 16.4 %convolution_convert_fusion.1 = bf16[1024,4608]{1,0:T(8,128)(2,1)} fusion(bf16[1024,1024]{1,0:T(8,128)(2,1)} %copy-done.14, bf16[1024,4608]{1,0:T(8,128)(2,1)} %get-tuple-element.25), kind=kOutput, calls=%fused_computation.6 | convolution fusion | flops 9668395008 | bytes 20971520 | tf_op jit(solution)/shard_map/dot_general | solution.py:28
  706.4 16.6 %convolution_convert_fusion = bf16[1024,4608]{1,0:T(8,128)(2,1)} fusion(bf16[1024,1024]{1,0:T(8,128)(2,1)} %copy-done.14, bf16[1024,4608]{1,0:T(8,128)(2,1)} %get-tuple-element.24), kind=kOutput, calls=%fused_computation.5 | convolution fusion | flops 9668395008 | bytes 20971520 | tf_op jit(solution)/shard_map/dot_general | solution.py:28
  723.1 17.1 %convolution_convert_fusion.2 = bf16[4608,1024]{1,0:T(8,128)(2,1)} fusion(bf16[1024,4608]{1,0:T(8,128)(2,1)} %get-tuple-element.26, bf16[1024,1024]{1,0:T(8,128)(2,1)} %bitcast_convert_fusion.1), kind=kOutput, calls=%fused_computation.7 | convolution fusion | flops 9668395008 | bytes 20971520 | tf_op jit(solution)/shard_map/dot_general | solution.py:28
  741.9 94.7 %reduce-scatter.9.cloned.1.call-done = bf16[128,3072]{1,0:T(8,128)(2,1)} async-done(((bf16[1024,3072]{1,0:T(8,128)(2,1)}), bf16[128,3072]{1,0:T(8,128)(2,1)}) %reduce-scatter.9.cloned.1.call-update) | async-done | bytes 786448 | tf_op jit(solution)/shard_map/reduce_scatter | solution.py:151
  836.7 166.0 %reduce-scatter.13.cloned.1.call-done = bf16[128,4608]{1,0:T(8,128)(2,1)} async-done(((bf16[1024,4608]{1,0:T(8,128)(2,1)}), bf16[128,4608]{1,0:T(8,128)(2,1)}) %reduce-scatter.13.cloned.1.call-update) | async-done | bytes 1179664 | tf_op jit(solution)/shard_map/reduce_scatter | solution.py:151
  1002.8 166.0 %reduce-scatter.15.cloned.1.call-done = bf16[128,4608]{1,0:T(8,128)(2,1)} async-done(((bf16[1024,4608]{1,0:T(8,128)(2,1)}), bf16[128,4608]{1,0:T(8,128)(2,1)}) %reduce-scatter.15.cloned.1.call-update) | async-done | bytes 1179664 | tf_op jit(solution)/shard_map/reduce_scatter | solution.py:151
  1168.8 165.8 %reduce-scatter.17.cloned.1.call-done = bf16[576,1024]{1,0:T(8,128)(2,1)} async-done(((bf16[4608,1024]{1,0:T(8,128)(2,1)}), bf16[576,1024]{1,0:T(8,128)(2,1)}) %reduce-scatter.17.cloned.1.call-update) | async-done | bytes 1179664 | tf_op jit(solution)/shard_map/reduce_scatter | solution.py:151
  1341.3 17.5 %convolution_add_fusion.1 = f32[1024,1024]{1,0:T(8,128)} fusion(f32[1024,1024]{1,0:T(8,128)} %copy-done.5, bf16[1024,4608]{1,0:T(8,128)(2,1)} %get-tuple-element.26, bf16[4608,1024]{1,0:T(8,128)(2,1)} %all-gather.31.cloned.1.call-done), kind=kOutput, calls=%fused_computation.66 | convolution fusion | flops 9664724992 | bytes 27262976 | tf_op jit(solution)/shard_map/dot_general | solution.py:40
  1358.7 40.1 %reduce-scatter.19.cloned.1.call-done = bf16[128,3]{1,0:T(8,128)(2,1)} async-done(((bf16[1024,3]{1,0:T(8,128)(2,1)}), bf16[128,3]{1,0:T(8,128)(2,1)}) %reduce-scatter.19.cloned.1.call-update) | async-done | bytes 784
  1418.3 19.6 %all-reduce.2 = (bf16[1024]{0:T(1024)(128)(2,1)S(1)}, bf16[1024]{0:T(1024)(128)(2,1)S(1)}) all-reduce(bf16[1024]{0:T(1024)(128)(2,1)S(1)} %get-tuple-element.15, bf16[1024]{0:T(1024)(128)(2,1)S(1)} %copy-done.31), channel_id=10, replica_groups=mesh['rep'=4,'fsdp'=8] {'fsdp'}, use_global_device_ids=true, to_apply=%region_6.7.clone | all-reduce | flops 2048 | bytes 8192
  1464.3 20.9 %all-gather.37.cloned.1.call-done = bf16[512,4608]{1,0:T(8,128)(2,1)} async-done(((bf16[128,4608]{1,0:T(8,128)(2,1)}), bf16[512,4608]{1,0:T(8,128)(2,1)}) %all-gather.37.cloned.1.call-update) | async-done | bytes 4718608 | tf_op jit(solution)/shard_map/all_gather | solution.py:13
  1489.9 34.1 %all-gather.39.cloned.1.call-done = bf16[512,4608]{1,0:T(8,128)(2,1)} async-done(((bf16[128,4608]{1,0:T(8,128)(2,1)}), bf16[512,4608]{1,0:T(8,128)(2,1)}) %all-gather.39.cloned.1.call-update) | async-done | bytes 4718608 | tf_op jit(solution)/shard_map/all_gather | solution.py:13
  1528.8 34.1 %all-gather.41.cloned.1.call-done = bf16[2304,1024]{1,0:T(8,128)(2,1)} async-done(((bf16[576,1024]{1,0:T(8,128)(2,1)}), bf16[2304,1024]{1,0:T(8,128)(2,1)}) %all-gather.41.cloned.1.call-update) | async-done | bytes 4718608 | tf_op jit(solution)/shard_map/all_gather | solution.py:13
  (189 shorter events, 191.5 us)
Async XLA Ops:
  7.2 104.9 %all-gather.23.cloned.1.call-start = ((), (), s32[]{:S(2)}) async-start(), calls=%async_computation.6 | async-start | bytes 7077888 | tf_op jit(solution)/shard_map/all_gather | solution.py:76
  8.0 153.8 %all-gather.25.cloned.1.call-start = ((), (), s32[]{:S(2)}) async-start(), calls=%async_computation.7 | async-start | bytes 2359296 | tf_op jit(solution)/shard_map/all_gather | solution.py:76
  8.7 291.8 %all-gather.27.cloned.1.call-start = ((), (), s32[]{:S(2)}) async-start(), calls=%async_computation.8 | async-start | bytes 10616832 | tf_op jit(solution)/shard_map/all_gather | solution.py:76
  9.4 429.4 %all-gather.29.cloned.1.call-start = ((), (), s32[]{:S(2)}) async-start(), calls=%async_computation.9 | async-start | bytes 10616832 | tf_op jit(solution)/shard_map/all_gather | solution.py:76
  10.0 567.1 %all-gather.31.cloned.1.call-start = ((), (), s32[]{:S(2)}) async-start(), calls=%async_computation.10 | async-start | bytes 10616832 | tf_op jit(solution)/shard_map/all_gather | solution.py:76
  10.6 730.8 %reduce-scatter.11.cloned.1.call-start = ((), (), s32[]{:S(2)}) async-start(), calls=%async_computation.12 | async-start | bytes 2359296 | tf_op jit(solution)/shard_map/reduce_scatter | solution.py:151
  10.7 63.3 %collective-permute-start = (bf16[16,2,1024]{2,1,0:T(2,128)(2,1)S(1)}, bf16[16,2,1024]{2,1,0:T(2,128)(2,1)S(1)}, u32[]{:S(2)}, u32[]{:S(2)}) collective-permute-start(bf16[16,2,1024]{2,1,0:T(2,128)(2,1)S(1)} %slice.59), channel_id=1, source_target_pairs={{0,1},{1,2},{2,3},{3,4},{4,5},{5,6},{6,7},{8,9},{9,10},{10,11},{11... | collective-permute-start | bytes 196616 | tf_op jit(solution)/shard_map/ppermute | solution.py:54
  39.2 85.9 %copy-start.22 = (f32[1024,1]{0,1:T(1,128)}, f32[1024,1]{0,1:T(1,128)S(1)}, u32[]{:S(2)}) copy-start(f32[1024,1]{0,1:T(1,128)S(1)} %get-tuple-element.34) | copy-start | bytes 12292
  39.2 85.9 %copy-start.24 = (f32[1024,1]{0,1:T(1,128)}, f32[1024,1]{0,1:T(1,128)S(1)}, u32[]{:S(2)}) copy-start(f32[1024,1]{0,1:T(1,128)S(1)} %get-tuple-element.35) | copy-start | bytes 12292
  39.3 85.9 %copy-start.26 = (f32[1024,1]{0,1:T(1,128)}, f32[1024,1]{0,1:T(1,128)S(1)}, u32[]{:S(2)}) copy-start(f32[1024,1]{0,1:T(1,128)S(1)} %get-tuple-element.36) | copy-start | bytes 12292
  168.8 131.7 %copy-start.14 = (bf16[1024,1024]{1,0:T(8,128)(2,1)}, bf16[1024,1024]{1,0:T(8,128)(2,1)S(1)}, u32[]{:S(2)}) copy-start(bf16[1024,1024]{1,0:T(8,128)(2,1)S(1)} %multiply_convert_fusion.7) | copy-start | bytes 6291460
  316.6 260.5 %copy-start.12 = (bf16[1024,1024]{1,0:T(8,128)(2,1)S(1)}, bf16[1024,1024]{1,0:T(8,128)(2,1)}, u32[]{:S(2)}) copy-start(bf16[1024,1024]{1,0:T(8,128)(2,1)} %bitcast_convert_fusion.1) | copy-start | bytes 6291460
  649.1 187.6 %reduce-scatter.9.cloned.1.call-start = ((), (), s32[]{:S(2)}) async-start(), calls=%async_computation.11 | async-start | bytes 7077888 | tf_op jit(solution)/shard_map/reduce_scatter | solution.py:151
  667.5 7.0 collective-permute-start.1
  689.9 312.8 %reduce-scatter.13.cloned.1.call-start = ((), (), s32[]{:S(2)}) async-start(), calls=%async_computation.13 | async-start | bytes 10616832 | tf_op jit(solution)/shard_map/reduce_scatter | solution.py:151
  706.4 462.4 %reduce-scatter.15.cloned.1.call-start = ((), (), s32[]{:S(2)}) async-start(), calls=%async_computation.14 | async-start | bytes 10616832 | tf_op jit(solution)/shard_map/reduce_scatter | solution.py:151
  723.1 611.5 %reduce-scatter.17.cloned.1.call-start = ((), (), s32[]{:S(2)}) async-start(), calls=%async_computation.15 | async-start | bytes 10616832 | tf_op jit(solution)/shard_map/reduce_scatter | solution.py:151
  740.3 594.4 %copy-start.37 = (u32[32]{0:T(128)S(1)}, u32[32]{0:T(128)}, u32[]{:S(2)}) copy-start(u32[32]{0:T(128)} %constant.35) | copy-start | bytes 388
  740.3 658.6 %reduce-scatter.19.cloned.1.call-start = ((), (), s32[]{:S(2)}) async-start(), calls=%async_computation.21 | async-start | bytes 294912
  741.3 716.9 %all-gather.35.cloned.1.call-start = ((), (), s32[]{:S(2)}) async-start(), calls=%async_computation.17 | async-start | bytes 1310720 | tf_op jit(solution)/shard_map/all_gather | solution.py:13
  741.9 718.6 %all-gather.33.cloned.1.call-start = ((), (), s32[]{:S(2)}) async-start(), calls=%async_computation.16 | async-start | bytes 3932160 | tf_op jit(solution)/shard_map/all_gather | solution.py:13
  836.7 648.5 %all-gather.37.cloned.1.call-start = ((), (), s32[]{:S(2)}) async-start(), calls=%async_computation.18 | async-start | bytes 5898240 | tf_op jit(solution)/shard_map/all_gather | solution.py:13
  1002.7 521.3 %all-gather.39.cloned.1.call-start = ((), (), s32[]{:S(2)}) async-start(), calls=%async_computation.19 | async-start | bytes 5898240 | tf_op jit(solution)/shard_map/all_gather | solution.py:13
  1168.8 394.2 %all-gather.41.cloned.1.call-start = ((), (), s32[]{:S(2)}) async-start(), calls=%async_computation.20 | async-start | bytes 5898240 | tf_op jit(solution)/shard_map/all_gather | solution.py:13
  (36 other events, 531.5 us)
Sparse Core Ops, SparseCore 0:
  10.2 101.8 all-gather.22
  114.2 47.4 all-gather.24
  163.9 136.5 all-gather.26
  302.6 136.2 all-gather.28
  440.9 136.2 all-gather.30
  649.2 66.8 reduce-scatter.10
  719.7 116.9 reduce-scatter.8
  840.2 162.4 reduce-scatter.12
  1006.3 162.3 reduce-scatter.14
  1172.2 162.3 reduce-scatter.16
  1338.5 60.3 reduce-scatter.18
  1400.3 15.7 all-gather.34
  1417.6 28.5 all-gather.32
  1447.6 37.4 all-gather.36
  1486.5 37.4 all-gather.38
  1525.5 37.4 all-gather.40
